TPU v7x, 128 devices: a whole 4x4x4 slice. The times are simulated.
128 devices in a mesh: ctx: 32 (over y, z, core), tp: 4 (over x).
Axes of the slice: x: 4, y: 4, z: 4, core: 2. Of those that a mesh axis runs over, the one named last changes fastest.
Arguments:
- tokens: bfloat16 [4096, 4096], P('ctx', 'tp'), may hold values from -6 to 6
- out_grad: bfloat16 [4096, 4096], P('ctx', 'tp'), may hold values from -4 to 4
- router_probs: bfloat16 [4096, 8], P('ctx'), may hold values from 0.049804688 to 0.5
- expert_ids: int32 [4096, 8], P('ctx'), may hold values from 0 to 63, all different within a row; in each aligned block of 128 rows (0 to 127, 128 to 255, ...) at most 24 rows name the same one
- w_gate: bfloat16 [64, 4096, 1536], P('ctx', None, 'tp'), may hold values from -0.09375 to 0.09375
- w_up: bfloat16 [64, 4096, 1536], P('ctx', None, 'tp'), may hold values from -0.09375 to 0.09375
- w_down: bfloat16 [64, 1536, 4096], P('ctx', 'tp'), may hold values from -0.15625 to 0.15625
Outputs:
- token_grad: bfloat16 [4096, 4096], P('ctx', 'tp')
- prob_grad: bfloat16 [4096, 8], P('ctx')
Inputs may be any that keep to these rules, and one draw needn't show every extreme that they name: `expert_ids`: each token names 8 different experts; among the 128 tokens of one index of ctx no expert is named by more than 24 tokens, a bound that some block reaches.
All inputs are finite; a program needn't handle non-finite values.
Results may differ from a plain program's by a relative error of at most 0.015.
Values may be sent and summed in bfloat16 or wider, within the bound.
A program may use at most 128 MiB of HBM per device.

v0:
```python
import jax
import jax.numpy as jnp
from jax import lax
from jax.sharding import PartitionSpec as P


def on_device(tokens, out_grad, router_probs, expert_ids, w_gate, w_up, w_down):
    groups = lax.axis_size("ctx")
    tok_rows, fanout = expert_ids.shape
    local_experts = w_gate.shape[0]
    experts_all = local_experts * groups
    capacity = 3 * tok_rows * fanout // (2 * experts_all)
    buffer_rows = experts_all * capacity
    flat_ids = expert_ids.reshape(tok_rows * fanout)
    expert_hot = (flat_ids[:, None] == jnp.arange(experts_all, dtype=jnp.int32)[None, :]).astype(
        jnp.int32
    )
    earlier = jnp.cumsum(expert_hot, axis=0) - expert_hot
    slot_index = jnp.sum(earlier * expert_hot, axis=1)
    target = flat_ids * capacity + slot_index
    row_hot = (target[:, None] == jnp.arange(buffer_rows, dtype=jnp.int32)[None, :]).astype(
        jnp.bfloat16
    )
    row_hot = row_hot.reshape(tok_rows, fanout, buffer_rows)
    selector = jnp.sum(row_hot, axis=1)
    prob_send = jnp.einsum("tkr,tk->r", row_hot, router_probs, preferred_element_type=jnp.float32)
    prob_send = prob_send.astype(jnp.bfloat16).reshape(groups, local_experts, capacity)

    def arrange(local_rows):
        placed = jnp.einsum("tr,td->rd", selector, local_rows, preferred_element_type=jnp.float32)
        return placed.astype(jnp.bfloat16).reshape(
            groups, local_experts, capacity, local_rows.shape[1]
        )

    full_tokens, full_grads = (
        lax.all_gather(tokens, "tp", axis=1, tiled=True),
        lax.all_gather(out_grad, "tp", axis=1, tiled=True),
    )
    x_rows, dy_rows, prob_rows = (
        lax.all_to_all(arrange(full_tokens), "ctx", split_axis=0, concat_axis=0, tiled=True),
        lax.all_to_all(arrange(full_grads), "ctx", split_axis=0, concat_axis=0, tiled=True),
        lax.all_to_all(prob_send, "ctx", split_axis=0, concat_axis=0, tiled=True),
    )
    gate_sum = jnp.einsum("secd,edf->secf", x_rows, w_gate, preferred_element_type=jnp.float32)
    up_sum = jnp.einsum("secd,edf->secf", x_rows, w_up, preferred_element_type=jnp.float32)
    down_back = jnp.einsum("secd,efd->secf", dy_rows, w_down, preferred_element_type=jnp.float32)
    sigmoid_gate = jax.nn.sigmoid(gate_sum)
    gated = gate_sum * sigmoid_gate
    hidden = gated * up_sum
    prob_part = jnp.sum(hidden * down_back, axis=3)
    prob_total = lax.psum(prob_part, "tp")
    hidden_grad = prob_rows.astype(jnp.float32)[..., None] * down_back
    gate_grad = (
        hidden_grad * up_sum * sigmoid_gate * (1.0 + gate_sum * (1.0 - sigmoid_gate))
    ).astype(jnp.bfloat16)
    up_grad = (hidden_grad * gated).astype(jnp.bfloat16)
    row_part = jnp.einsum("secf,edf->secd", gate_grad, w_gate, preferred_element_type=jnp.float32)
    row_part = row_part + jnp.einsum(
        "secf,edf->secd", up_grad, w_up, preferred_element_type=jnp.float32
    )
    row_grads = lax.psum_scatter(
        row_part.astype(jnp.bfloat16), "tp", scatter_dimension=3, tiled=True
    )
    back_rows, back_probs = (
        lax.all_to_all(row_grads, "ctx", split_axis=0, concat_axis=0, tiled=True),
        lax.all_to_all(
            prob_total.astype(jnp.bfloat16), "ctx", split_axis=0, concat_axis=0, tiled=True
        ),
    )
    token_grad = jnp.einsum(
        "tr,rd->td",
        selector,
        back_rows.reshape(buffer_rows, back_rows.shape[3]),
        preferred_element_type=jnp.float32,
    )
    prob_grad = back_probs.reshape(buffer_rows)[target].reshape(tok_rows, fanout)
    return (token_grad.astype(jnp.bfloat16), prob_grad)


def solution(mesh):
    return jax.shard_map(
        on_device,
        mesh=mesh,
        in_specs=(
            P("ctx", "tp"),
            P("ctx", "tp"),
            P("ctx", None),
            P("ctx", None),
            P("ctx", None, "tp"),
            P("ctx", None, "tp"),
            P("ctx", "tp", None),
        ),
        out_specs=(P("ctx", "tp"), P("ctx", None)),
        check_vma=False,
    )
```

profile of v0, /device:TPU:1, one launch (start us, length us, event | category | flops | bytes accessed | tf_op | source)
XLA Modules:
  0.0 695.2 jit_solution(9516662253684740646)
XLA Ops:
  7.2 0.0 all-gather.5.cloned.1.call-start
  7.2 0.7 all-gather.5.cloned.1.call-update
  7.9 0.8 copy.72
  8.7 0.1 eq.44
  8.8 0.1 eq.40
  8.9 0.8 copy.86
  9.7 18.0 %reduce-window.6 = s32[64,8,128]{2,1,0:T(8,128)S(1)} reduce-window(s32[64,8,128]{2,1,0:T(8,128)S(1)} %fusion.34, s32[]{:T(128)} %constant.4.clone.1), window={size=1x1x128 pad=0_0x0_0x127_0}, to_apply=%region_0.0 | reduce-window | flops 8323072 | bytes 524292 | tf_op jit(solution)/shard_map/reduce-window
  27.7 0.1 slice.10
  27.8 0.1 copy.75
  28.0 0.1 copy.76
  28.1 0.1 broadcast_add_fusion
  28.3 0.1 fusion.33
  28.3 0.1 reduce_sum.35
  28.4 0.6 broadcast_multiply_fusion
  29.1 1.2 fusion.30
  30.3 0.7 reshape.92
  31.0 9.6 %all-to-all-start = ((bf16[32,2,24]{2,1,0:T(2,128)(2,1)}), bf16[32,2,24]{2,1,0:T(2,128)(2,1)S(1)}, u32[]{:S(2)}, u32[]{:S(2)}) async-start(bf16[32,2,24]{2,1,0:T(2,128)(2,1)} %reshape.92), calls=%async_computation | async-start | bytes 32768 | tf_op jit(solution)/shard_map/all_to_all | solution.py:42
  40.6 3.1 fusion.15
  43.7 0.0 all-gather.5.cloned.1.call-done
  43.8 7.5 %convolution_convert_fusion = bf16[1536,4096]{1,0:T(8,128)(2,1)} fusion(bf16[128,1536]{1,0:T(8,128)(2,1)S(1)} %fusion.15, bf16[128,4096]{1,0:T(8,128)(2,1)} %all-gather.5.cloned.1.call-done), kind=kOutput, calls=%fused_computation.2 | convolution fusion | flops 1616904192 | bytes 14024704 | tf_op jit(solution)/shard_map/tr,td->rd/dot_general | solution.py:30
  51.3 0.0 all-to-all-done
  51.3 7.4 %all-to-all-start.2 = ((bf16[32,2,24,4096]{3,2,1,0:T(8,128)(2,1)}), bf16[32,2,24,4096]{3,2,1,0:T(8,128)(2,1)}, u32[]{:S(2)}, u32[]{:S(2)}) async-start(bf16[32,2,24,4096]{3,2,1,0:T(8,128)(2,1)} %bitcast.101), calls=%async_computation.2 | async-start | bytes 25165824 | tf_op jit(solution)/shard_map/all_to_all | solution.py:40
  58.7 0.0 all-gather.3.cloned.1.call-start
  58.8 0.7 all-gather.3.cloned.1.call-update
  59.5 25.8 %all-gather.3.cloned.1.call-done = bf16[128,4096]{1,0:T(8,128)(2,1)} async-done(((bf16[128,1024]{1,0:T(8,128)(2,1)}), bf16[128,4096]{1,0:T(8,128)(2,1)}) %all-gather.3.cloned.1.call-update) | async-done | bytes 1048592 | tf_op jit(solution)/shard_map/all_gather | solution.py:37
  85.3 7.6 %convolution_convert_fusion.1 = bf16[1536,4096]{1,0:T(8,128)(2,1)} fusion(bf16[128,1536]{1,0:T(8,128)(2,1)S(1)} %fusion.15, bf16[128,4096]{1,0:T(8,128)(2,1)} %all-gather.3.cloned.1.call-done), kind=kOutput, calls=%fused_computation.3 | convolution fusion | flops 1616904192 | bytes 14024704 | tf_op jit(solution)/shard_map/tr,td->rd/dot_general | solution.py:30
  92.9 140.5 %all-to-all-done.2 = bf16[32,2,24,4096]{3,2,1,0:T(8,128)(2,1)} async-done(((bf16[32,2,24,4096]{3,2,1,0:T(8,128)(2,1)}), bf16[32,2,24,4096]{3,2,1,0:T(8,128)(2,1)}, u32[]{:S(2)}, u32[]{:S(2)}) %all-to-all-start.2) | async-done | bytes 12582944 | tf_op jit(solution)/shard_map/all_to_all | solution.py:40
  233.4 29.7 %all-to-all-start.1 = ((bf16[32,2,24,4096]{3,2,1,0:T(8,128)(2,1)}), bf16[32,2,24,4096]{3,2,1,0:T(8,128)(2,1)}, u32[]{:S(2)}, u32[]{:S(2)}) async-start(bf16[32,2,24,4096]{3,2,1,0:T(8,128)(2,1)} %bitcast.102), calls=%async_computation.1 | async-start | bytes 25165824 | tf_op jit(solution)/shard_map/all_to_all | solution.py:41
  263.1 0.2 reduce-scatter.2.cloned.1.call-start
  263.3 0.1 copy.77
  263.4 0.1 copy.78
  263.5 11.1 %fusion.3 = f32[2,32,24,384]{3,2,1,0:T(8,128)S(1)} fusion(bf16[32,2,24,4096]{3,2,1,0:T(8,128)(2,1)} %all-to-all-done.2, bf16[2,4096,384]{2,1,0:T(8,128)(2,1)} %param.11), kind=kOutput, calls=%fused_computation.7 | convolution fusion | flops 4831838208 | bytes 21233664 | tf_op jit(solution)/shard_map/secd,edf->secf/dot_general | solution.py:44
  274.5 163.2 %all-to-all-done.1 = bf16[32,2,24,4096]{3,2,1,0:T(8,128)(2,1)} async-done(((bf16[32,2,24,4096]{3,2,1,0:T(8,128)(2,1)}), bf16[32,2,24,4096]{3,2,1,0:T(8,128)(2,1)}, u32[]{:S(2)}, u32[]{:S(2)}) %all-to-all-start.1) | async-done | bytes 12582944 | tf_op jit(solution)/shard_map/all_to_all | solution.py:41
  437.7 11.1 %fusion.1 = f32[2,32,24,384]{3,2,1,0:T(8,128)S(1)} fusion(bf16[32,2,24,4096]{3,2,1,0:T(8,128)(2,1)} %all-to-all-done.1, bf16[2,384,4096]{2,1,0:T(8,128)(2,1)} %param.13), kind=kOutput, calls=%fused_computation.5 | convolution fusion | flops 4831838208 | bytes 21233664 | tf_op jit(solution)/shard_map/secd,efd->secf/dot_general | solution.py:46
  448.8 0.0 copy-start
  448.8 13.6 %fusion.25 = (f32[32,2,24]{2,0,1:T(8,128)S(1)}, f32[2,32,24,384]{3,2,1,0:T(8,128)}) fusion(f32[2,32,24,384]{3,2,1,0:T(8,128)S(1)} %fusion.1, f32[2,32,24,384]{3,2,1,0:T(8,128)S(1)} %fusion.3, bf16[2,4096,384]{2,1,0:T(8,128)(2,1)} %param.12, bf16[32,2,24,4096]{3,2,1,0:T(8,128)(2,1)} %all-to-all-done.2), kind=kOutput, calls=%fused_computation.35 | convolution fusion | flops 4835965440 | bytes 25958400 | tf_op jit(solution)/shard_map/secd,edf->secf/dot_general | solution.py:45
  462.5 0.0 copy-done
  462.5 16.0 %fusion.7 = f32[2,32,24,4096]{3,2,1,0:T(8,128)} fusion(bf16[2,4096,384]{2,1,0:T(8,128)(2,1)} %param.11, f32[2,32,24,384]{3,2,1,0:T(8,128)S(1)} %fusion.3, f32[2,32,24,384]{3,2,1,0:T(8,128)} %get-tuple-element.17, f32[2,32,24,384]{3,2,1,0:T(8,128)} %copy-done, f32[32,2,24]{2,0,1:T(8,128)S(1)} %copy.78), kind=kOutput, calls=%fused_computation.11 | convolution fusion | flops 4838326272 | bytes 38541312 | tf_op jit(solution)/shard_map/secf,edf->secd/dot_general | solution.py:57
  478.4 19.0 %fusion = bf16[32,2,24,4096]{3,2,0,1:T(8,128)(2,1)} fusion(f32[2,32,24,4096]{3,2,1,0:T(8,128)} %fusion.7, bf16[2,4096,384]{2,1,0:T(8,128)(2,1)} %param.12, f32[2,32,24,384]{3,2,1,0:T(8,128)} %copy-done, f32[32,2,24]{2,0,1:T(8,128)S(1)} %copy.78, f32[2,32,24,384]{3,2,1,0:T(8,128)S(1)} %fusion.3), kind=kOutput, calls=%fused_computation.4 | convolution fusion | flops 4848549888 | bytes 48764928 | tf_op jit(solution)/shard_map/secf,edf->secd/dot_general | solution.py:58
  497.4 0.0 reduce-scatter.2.cloned.1.call-update
  497.4 0.1 copy.83
  497.5 13.3 %psum.7 = bf16[32,2,24]{0,2,1:T(8,128)(2,1)S(1)} all-reduce(f32[32,2,24]{0,2,1:T(8,128)S(1)} %copy.83), channel_id=1, replica_groups=mesh['ctx'=32,'tp'=4] {'tp'}, use_global_device_ids=true, to_apply=%region_6.7 | all-reduce | flops 1536 | bytes 9216 | tf_op jit(solution)/shard_map/psum | solution.py:51
  510.8 0.7 copy.84
  511.5 33.5 %all-to-all-start.4 = ((bf16[32,2,24]{2,1,0:T(2,128)(2,1)}), bf16[32,2,24]{2,1,0:T(2,128)(2,1)S(1)}, u32[]{:S(2)}, u32[]{:S(2)}) async-start(bf16[32,2,24]{2,1,0:T(2,128)(2,1)} %copy.84), calls=%async_computation.5 | async-start | bytes 32768 | tf_op jit(solution)/shard_map/all_to_all | solution.py:66
  545.0 90.3 %reduce-scatter.2.cloned.1.call-done = bf16[32,2,24,1024]{3,2,0,1:T(8,128)(2,1)} async-done(((bf16[32,2,24,4096]{3,2,0,1:T(8,128)(2,1)}), bf16[32,2,24,1024]{3,2,0,1:T(8,128)(2,1)}) %reduce-scatter.2.cloned.1.call-update) | async-done | bytes 3145744 | tf_op jit(solution)/shard_map/reduce_scatter | solution.py:61
  635.3 4.0 copy.82
  639.3 0.0 all-to-all-done.4
  639.3 0.0 copy-start.1
  639.3 0.6 copy-done.1
  639.9 7.6 %all-to-all-start.3 = ((bf16[32,2,24,1024]{3,2,1,0:T(8,128)(2,1)}), bf16[32,2,24,1024]{3,2,1,0:T(8,128)(2,1)S(1)}, u32[]{:S(2)}, u32[]{:S(2)}) async-start(bf16[32,2,24,1024]{3,2,1,0:T(8,128)(2,1)} %copy.82), calls=%async_computation.4 | async-start | bytes 6291456 | tf_op jit(solution)/shard_map/all_to_all | solution.py:65
  647.6 0.9 mul.67
  648.5 0.8 reshape.96
  649.3 6.8 gather_fusion
  656.2 0.7 reshape.97
  656.9 1.4 copy.85
  658.3 29.1 %all-to-all-done.3 = bf16[32,2,24,1024]{3,2,1,0:T(8,128)(2,1)S(1)} async-done(((bf16[32,2,24,1024]{3,2,1,0:T(8,128)(2,1)}), bf16[32,2,24,1024]{3,2,1,0:T(8,128)(2,1)S(1)}, u32[]{:S(2)}, u32[]{:S(2)}) %all-to-all-start.3) | async-done | bytes 3145760 | tf_op jit(solution)/shard_map/all_to_all | solution.py:65
  687.3 1.3 convolution_convert_fusion.2
  (5 shorter events, 0.1 us)
Async XLA Ops:
  7.2 36.6 %all-gather.5.cloned.1.call-start = ((), (), s32[]{:S(2)}) async-start(), calls=%async_computation.7 | async-start | bytes 1310720 | tf_op jit(solution)/shard_map/all_gather | solution.py:36
  31.0 20.3 %all-to-all-start = ((bf16[32,2,24]{2,1,0:T(2,128)(2,1)}), bf16[32,2,24]{2,1,0:T(2,128)(2,1)S(1)}, u32[]{:S(2)}, u32[]{:S(2)}) async-start(bf16[32,2,24]{2,1,0:T(2,128)(2,1)} %reshape.92), calls=%async_computation | async-start | bytes 32768 | tf_op jit(solution)/shard_map/all_to_all | solution.py:42
  51.3 182.1 %all-to-all-start.2 = ((bf16[32,2,24,4096]{3,2,1,0:T(8,128)(2,1)}), bf16[32,2,24,4096]{3,2,1,0:T(8,128)(2,1)}, u32[]{:S(2)}, u32[]{:S(2)}) async-start(bf16[32,2,24,4096]{3,2,1,0:T(8,128)(2,1)} %bitcast.101), calls=%async_computation.2 | async-start | bytes 25165824 | tf_op jit(solution)/shard_map/all_to_all | solution.py:40
  58.7 26.6 %all-gather.3.cloned.1.call-start = ((), (), s32[]{:S(2)}) async-start(), calls=%async_computation.6 | async-start | bytes 1310720 | tf_op jit(solution)/shard_map/all_gather | solution.py:37
  233.4 204.3 %all-to-all-start.1 = ((bf16[32,2,24,4096]{3,2,1,0:T(8,128)(2,1)}), bf16[32,2,24,4096]{3,2,1,0:T(8,128)(2,1)}, u32[]{:S(2)}, u32[]{:S(2)}) async-start(bf16[32,2,24,4096]{3,2,1,0:T(8,128)(2,1)} %bitcast.102), calls=%async_computation.1 | async-start | bytes 25165824 | tf_op jit(solution)/shard_map/all_to_all | solution.py:41
  263.1 372.2 %reduce-scatter.2.cloned.1.call-start = ((), (), s32[]{:S(2)}) async-start(), calls=%async_computation.8 | async-start | bytes 15728640 | tf_op jit(solution)/shard_map/reduce_scatter | solution.py:61
  448.8 13.7 %copy-start = (f32[2,32,24,384]{3,2,1,0:T(8,128)}, f32[2,32,24,384]{3,2,1,0:T(8,128)S(1)}, u32[]{:S(2)}) copy-start(f32[2,32,24,384]{3,2,1,0:T(8,128)S(1)} %fusion.1) | copy-start | bytes 7077892
  511.5 127.8 %all-to-all-start.4 = ((bf16[32,2,24]{2,1,0:T(2,128)(2,1)}), bf16[32,2,24]{2,1,0:T(2,128)(2,1)S(1)}, u32[]{:S(2)}, u32[]{:S(2)}) async-start(bf16[32,2,24]{2,1,0:T(2,128)(2,1)} %copy.84), calls=%async_computation.5 | async-start | bytes 32768 | tf_op jit(solution)/shard_map/all_to_all | solution.py:66
  639.3 0.6 copy-start.1
  639.9 47.4 %all-to-all-start.3 = ((bf16[32,2,24,1024]{3,2,1,0:T(8,128)(2,1)}), bf16[32,2,24,1024]{3,2,1,0:T(8,128)(2,1)S(1)}, u32[]{:S(2)}, u32[]{:S(2)}) async-start(bf16[32,2,24,1024]{3,2,1,0:T(8,128)(2,1)} %copy.82), calls=%async_computation.4 | async-start | bytes 6291456 | tf_op jit(solution)/shard_map/all_to_all | solution.py:65
Sparse Core Ops, SparseCore 0:
  9.7 26.2 all-gather.4
  61.3 23.9 all-gather.2
  497.5 137.7 reduce-scatter.1
where the time goes:
time: 696 us; the launch traced here: 695 us
  waiting for transfers between devices  450 us (65%)
  matrix products  88.4 us (13%)
  starting transfers between devices  88.1 us (13%)
  other arithmetic  22 us (3%)
  local copies, waits for them, and re-layouts  19.1 us (3%)
  between operations  13.9 us (2%)
  blocking collectives  13.3 us (2%)
    all_to_all x1, waiting for transfers between devices, on_device(): lax.all_to_all(arrange(full_grads), 'ctx', split_axis=0, concat_axis=0, t...  163 us
    all_to_all x1, waiting for transfers between devices, on_device(): lax.all_to_all(arrange(full_tokens), 'ctx', split_axis=0, concat_axis=0,...  140 us
    reduce_scatter x1, waiting for transfers between devices, on_device(): lax.psum_scatter(row_part.astype(jnp.bfloat16), 'tp', scatter_dimension=3...  90.3 us
    all_to_all x1, starting transfers between devices, on_device(): lax.all_to_all(prob_total.astype(jnp.bfloat16), 'ctx', split_axis=0, conc...  33.5 us
    all_to_all x1, starting transfers between devices, on_device(): lax.all_to_all(arrange(full_grads), 'ctx', split_axis=0, concat_axis=0, t...  29.7 us
    all_to_all x1, waiting for transfers between devices, on_device(): lax.all_to_all(row_grads, 'ctx', split_axis=0, concat_axis=0, tiled=True)  29.1 us
    all_gather x1, waiting for transfers between devices, on_device(): lax.all_gather(out_grad, 'tp', axis=1, tiled=True)  25.8 us
    dot_general x1, matrix products, on_device(): jnp.einsum('secf,edf->secd', up_grad, w_up, preferred_element_type=jnp.fl...  19 us
  transfers between devices with their start and end apart: 8, of which 5 were waited for; matrix products, arithmetic and copies ran while one was open for 10% of the time, Pallas kernels for 0%

commit v1 on v0

--- a/solution.py
+++ b/solution.py
@@ -2,6 +2,19 @@
 import jax.numpy as jnp
 from jax import lax
 from jax.sharding import PartitionSpec as P
+
+
+def ring_gather(x, axis, dim):
+    ways = lax.axis_size(axis)
+    up = [(d, (d + 1) % ways) for d in range(ways)]
+    down = [(d, (d - 1) % ways) for d in range(ways)]
+    earlier, later = ([x], [x])
+    for _ in range(ways // 2):
+        earlier.append(lax.ppermute(earlier[-1], axis, up))
+    for _ in range((ways - 1) // 2):
+        later.append(lax.ppermute(later[-1], axis, down))
+    line = jnp.concatenate([*earlier[::-1], *later[1:]], axis=dim)
+    return jnp.roll(line, (lax.axis_index(axis) - ways // 2) * x.shape[dim], axis=dim)
 
 
 def on_device(tokens, out_grad, router_probs, expert_ids, w_gate, w_up, w_down):
@@ -34,7 +47,7 @@
 
     full_tokens, full_grads = (
         lax.all_gather(tokens, "tp", axis=1, tiled=True),
-        lax.all_gather(out_grad, "tp", axis=1, tiled=True),
+        ring_gather(out_grad, "tp", 1),
     )
     x_rows, dy_rows, prob_rows = (
         lax.all_to_all(arrange(full_tokens), "ctx", split_axis=0, concat_axis=0, tiled=True),

time: 696 us -> 697 us (level)
    all_gather x1 -> x0, waiting for transfers between devices: 25.8 us -> none  [on_device(): lax.all_gather(out_grad, 'tp', axis=1, tiled=True)]
    all_gather x1, waiting for transfers between devices: 0.02 us -> 25.7 us  [on_device(): lax.all_gather(tokens, 'tp', axis=1, tiled=True)]
    all_to_all x1, waiting for transfers between devices: 163 us -> 141 us  [on_device(): lax.all_to_all(arrange(full_grads), 'ctx', split_axis=0, concat_axis=0, t...]
    all_to_all x1, starting transfers between devices: 7.43 us -> 29.7 us  [on_device(): lax.all_to_all(arrange(full_tokens), 'ctx', split_axis=0, concat_axis=0,...]
    all_to_all x1, starting transfers between devices: 29.7 us -> 7.44 us  [on_device(): lax.all_to_all(arrange(full_grads), 'ctx', split_axis=0, concat_axis=0, t...]
    all_to_all x1, waiting for transfers between devices: 140 us -> 162 us  [on_device(): lax.all_to_all(arrange(full_tokens), 'ctx', split_axis=0, concat_axis=0,...]
  transfers between devices with their start and end apart: 8 -> 10, of which waited for: 5 -> 5; matrix products, arithmetic and copies ran while one was open for 10% -> 10% of each run, Pallas kernels for 0% -> 0%
where the time goes in v1:
time: 697 us
  waiting for transfers between devices  448 us (64%)
  starting transfers between devices  91.8 us (13%)
  matrix products  87.1 us (12%)
  other arithmetic  22 us (3%)
  local copies, waits for them, and re-layouts  19.3 us (3%)
  between operations  14.3 us (2%)
  blocking collectives  13.5 us (2%)
    all_to_all x1, waiting for transfers between devices, on_device(): lax.all_to_all(arrange(full_tokens), 'ctx', split_axis=0, concat_axis=0,...  162 us
    all_to_all x1, waiting for transfers between devices, on_device(): lax.all_to_all(arrange(full_grads), 'ctx', split_axis=0, concat_axis=0, t...  141 us
    reduce_scatter x1, waiting for transfers between devices, on_device(): lax.psum_scatter(row_part.astype(jnp.bfloat16), 'tp', scatter_dimension=3...  90 us
    all_to_all x1, starting transfers between devices, on_device(): lax.all_to_all(prob_total.astype(jnp.bfloat16), 'ctx', split_axis=0, conc...  33.5 us
    all_to_all x1, starting transfers between devices, on_device(): lax.all_to_all(arrange(full_tokens), 'ctx', split_axis=0, concat_axis=0,...  29.7 us
    all_to_all x1, waiting for transfers between devices, on_device(): lax.all_to_all(row_grads, 'ctx', split_axis=0, concat_axis=0, tiled=True)  29.1 us
    all_gather x1, waiting for transfers between devices, on_device(): lax.all_gather(tokens, 'tp', axis=1, tiled=True)  25.7 us
    dot_general x1, matrix products, on_device(): jnp.einsum('secf,edf->secd', up_grad, w_up, preferred_element_type=jnp.fl...  18.9 us
  transfers between devices with their start and end apart: 10, of which 5 were waited for; matrix products, arithmetic and copies ran while one was open for 10% of the time, Pallas kernels for 0%

profile of v1, /device:TPU:1, one launch (start us, length us, event | category | flops | bytes accessed | tf_op | source)
XLA Modules:
  0.0 696.6 jit_solution(18338977923162300880)
XLA Ops:
  7.2 0.0 copy-start.3
  7.2 2.1 collective-permute-start
  9.3 1.4 collective-permute-start.2
  10.6 0.8 copy.72
  11.4 0.1 eq.47
  11.5 0.1 eq.43
  11.6 18.0 %reduce-window.6 = s32[64,8,128]{2,1,0:T(8,128)S(1)} reduce-window(s32[64,8,128]{2,1,0:T(8,128)S(1)} %fusion.35, s32[]{:T(128)} %constant.36.clone.1), window={size=1x1x128 pad=0_0x0_0x127_0}, to_apply=%region_0.0 | reduce-window | flops 8323072 | bytes 524292 | tf_op jit(solution)/shard_map/reduce-window
  29.6 0.1 slice.10
  29.8 0.1 copy.75
  30.0 0.1 copy.76
  30.1 0.1 broadcast_add_fusion
  30.2 0.1 fusion.34
  30.3 0.0 copy-done.3
  30.3 0.1 copy.86
  30.4 0.1 reduce_sum.35
  30.5 0.6 broadcast_multiply_fusion
  31.1 0.0 collective-permute-done
  31.1 0.1 collective-permute-start.1
  31.3 0.0 copy-start.1
  31.3 1.2 fusion.30
  32.5 0.7 reshape.92
  33.2 9.7 %all-to-all-start = ((bf16[32,2,24]{2,1,0:T(2,128)(2,1)}), bf16[32,2,24]{2,1,0:T(2,128)(2,1)}, u32[]{:S(2)}, u32[]{:S(2)}) async-start(bf16[32,2,24]{2,1,0:T(2,128)(2,1)} %reshape.92), calls=%async_computation | async-start | bytes 32768 | tf_op jit(solution)/shard_map/all_to_all | solution.py:55
  42.9 3.1 fusion.15
  46.0 0.0 collective-permute-done.1
  46.1 0.0 copy-done.1
  46.1 0.0 collective-permute-done.2
  46.3 6.3 convolution_convert_fusion.1
  52.6 0.0 all-to-all-done
  52.6 7.4 %all-to-all-start.1 = ((bf16[32,2,24,4096]{3,2,1,0:T(8,128)(2,1)}), bf16[32,2,24,4096]{3,2,1,0:T(8,128)(2,1)}, u32[]{:S(2)}, u32[]{:S(2)}) async-start(bf16[32,2,24,4096]{3,2,1,0:T(8,128)(2,1)} %bitcast.100), calls=%async_computation.1 | async-start | bytes 25165824 | tf_op jit(solution)/shard_map/all_to_all | solution.py:54
  60.0 0.0 all-gather.2.cloned.1.call-start
  60.1 0.7 all-gather.2.cloned.1.call-update
  60.8 25.7 %all-gather.2.cloned.1.call-done = bf16[128,4096]{1,0:T(8,128)(2,1)} async-done(((bf16[128,1024]{1,0:T(8,128)(2,1)}), bf16[128,4096]{1,0:T(8,128)(2,1)}) %all-gather.2.cloned.1.call-update) | async-done | bytes 1048592 | tf_op jit(solution)/shard_map/all_gather | solution.py:49
  86.5 7.6 %convolution_convert_fusion = bf16[1536,4096]{1,0:T(8,128)(2,1)} fusion(bf16[128,1536]{1,0:T(8,128)(2,1)S(1)} %fusion.15, bf16[128,4096]{1,0:T(8,128)(2,1)} %all-gather.2.cloned.1.call-done), kind=kOutput, calls=%fused_computation.2 | convolution fusion | flops 1616904192 | bytes 14024704 | tf_op jit(solution)/shard_map/tr,td->rd/dot_general | solution.py:43
  94.2 140.6 %all-to-all-done.1 = bf16[32,2,24,4096]{3,2,1,0:T(8,128)(2,1)} async-done(((bf16[32,2,24,4096]{3,2,1,0:T(8,128)(2,1)}), bf16[32,2,24,4096]{3,2,1,0:T(8,128)(2,1)}, u32[]{:S(2)}, u32[]{:S(2)}) %all-to-all-start.1) | async-done | bytes 12582944 | tf_op jit(solution)/shard_map/all_to_all | solution.py:54
  234.7 29.7 %all-to-all-start.2 = ((bf16[32,2,24,4096]{3,2,1,0:T(8,128)(2,1)}), bf16[32,2,24,4096]{3,2,1,0:T(8,128)(2,1)}, u32[]{:S(2)}, u32[]{:S(2)}) async-start(bf16[32,2,24,4096]{3,2,1,0:T(8,128)(2,1)} %bitcast.101), calls=%async_computation.2 | async-start | bytes 25165824 | tf_op jit(solution)/shard_map/all_to_all | solution.py:53
  264.4 0.2 reduce-scatter.2.cloned.1.call-start
  264.6 0.8 copy.77
  265.4 0.1 copy.78
  265.5 11.1 %fusion.1 = f32[2,32,24,384]{3,2,1,0:T(8,128)S(1)} fusion(bf16[32,2,24,4096]{3,2,1,0:T(8,128)(2,1)} %all-to-all-done.1, bf16[2,384,4096]{2,1,0:T(8,128)(2,1)} %param.13), kind=kOutput, calls=%fused_computation.5 | convolution fusion | flops 4831838208 | bytes 21233664 | tf_op jit(solution)/shard_map/secd,efd->secf/dot_general | solution.py:59
  276.6 162.4 %all-to-all-done.2 = bf16[32,2,24,4096]{3,2,1,0:T(8,128)(2,1)} async-done(((bf16[32,2,24,4096]{3,2,1,0:T(8,128)(2,1)}), bf16[32,2,24,4096]{3,2,1,0:T(8,128)(2,1)}, u32[]{:S(2)}, u32[]{:S(2)}) %all-to-all-start.2) | async-done | bytes 12582944 | tf_op jit(solution)/shard_map/all_to_all | solution.py:53
  439.0 11.1 %fusion.3 = f32[2,32,24,384]{3,2,1,0:T(8,128)S(1)} fusion(bf16[32,2,24,4096]{3,2,1,0:T(8,128)(2,1)} %all-to-all-done.2, bf16[2,4096,384]{2,1,0:T(8,128)(2,1)} %param.11), kind=kOutput, calls=%fused_computation.7 | convolution fusion | flops 4831838208 | bytes 21233664 | tf_op jit(solution)/shard_map/secd,edf->secf/dot_general | solution.py:57
  450.1 0.0 copy-start
  450.1 13.7 %fusion.25 = (f32[32,2,24]{2,0,1:T(8,128)S(1)}, f32[2,32,24,384]{3,2,1,0:T(8,128)}) fusion(f32[2,32,24,384]{3,2,1,0:T(8,128)S(1)} %fusion.1, f32[2,32,24,384]{3,2,1,0:T(8,128)S(1)} %fusion.3, bf16[2,4096,384]{2,1,0:T(8,128)(2,1)} %param.12, bf16[32,2,24,4096]{3,2,1,0:T(8,128)(2,1)} %all-to-all-done.2), kind=kOutput, calls=%fused_computation.35 | convolution fusion | flops 4835965440 | bytes 25958400 | tf_op jit(solution)/shard_map/secd,edf->secf/dot_general | solution.py:58
  463.8 0.0 copy-done
  463.8 15.8 %fusion.7 = f32[2,32,24,4096]{3,2,1,0:T(8,128)} fusion(bf16[2,4096,384]{2,1,0:T(8,128)(2,1)} %param.11, f32[2,32,24,384]{3,2,1,0:T(8,128)} %copy-done, f32[2,32,24,384]{3,2,1,0:T(8,128)} %get-tuple-element.17, f32[2,32,24,384]{3,2,1,0:T(8,128)S(1)} %fusion.1, f32[32,2,24]{2,0,1:T(8,128)S(1)} %copy.78), kind=kOutput, calls=%fused_computation.11 | convolution fusion | flops 4838326272 | bytes 38541312 | tf_op jit(solution)/shard_map/secf,edf->secd/dot_general | solution.py:70
  479.7 18.9 %fusion = bf16[32,2,24,4096]{3,2,0,1:T(8,128)(2,1)} fusion(f32[2,32,24,4096]{3,2,1,0:T(8,128)} %fusion.7, bf16[2,4096,384]{2,1,0:T(8,128)(2,1)} %param.12, f32[2,32,24,384]{3,2,1,0:T(8,128)S(1)} %fusion.1, f32[32,2,24]{2,0,1:T(8,128)S(1)} %copy.78, f32[2,32,24,384]{3,2,1,0:T(8,128)} %copy-done), kind=kOutput, calls=%fused_computation.4 | convolution fusion | flops 4848549888 | bytes 48764928 | tf_op jit(solution)/shard_map/secf,edf->secd/dot_general | solution.py:71
  498.6 0.0 reduce-scatter.2.cloned.1.call-update
  498.6 0.1 copy.83
  498.7 13.5 %psum.7 = bf16[32,2,24]{0,2,1:T(8,128)(2,1)S(1)} all-reduce(f32[32,2,24]{0,2,1:T(8,128)S(1)} %copy.83), channel_id=1, replica_groups=mesh['ctx'=32,'tp'=4] {'tp'}, use_global_device_ids=true, to_apply=%region_6.7 | all-reduce | flops 1536 | bytes 9216 | tf_op jit(solution)/shard_map/psum | solution.py:64
  512.2 0.7 copy.84
  512.9 33.5 %all-to-all-start.4 = ((bf16[32,2,24]{2,1,0:T(2,128)(2,1)}), bf16[32,2,24]{2,1,0:T(2,128)(2,1)S(1)}, u32[]{:S(2)}, u32[]{:S(2)}) async-start(bf16[32,2,24]{2,1,0:T(2,128)(2,1)} %copy.84), calls=%async_computation.5 | async-start | bytes 32768 | tf_op jit(solution)/shard_map/all_to_all | solution.py:79
  546.4 90.0 %reduce-scatter.2.cloned.1.call-done = bf16[32,2,24,1024]{3,2,0,1:T(8,128)(2,1)} async-done(((bf16[32,2,24,4096]{3,2,0,1:T(8,128)(2,1)}), bf16[32,2,24,1024]{3,2,0,1:T(8,128)(2,1)}) %reduce-scatter.2.cloned.1.call-update) | async-done | bytes 3145744 | tf_op jit(solution)/shard_map/reduce_scatter | solution.py:74
  636.4 4.0 copy.82
  640.4 0.0 all-to-all-done.4
  640.4 0.0 copy-start.2
  640.4 0.6 copy-done.2
  641.0 7.7 %all-to-all-start.3 = ((bf16[32,2,24,1024]{3,2,1,0:T(8,128)(2,1)}), bf16[32,2,24,1024]{3,2,1,0:T(8,128)(2,1)S(1)}, u32[]{:S(2)}, u32[]{:S(2)}) async-start(bf16[32,2,24,1024]{3,2,1,0:T(8,128)(2,1)} %copy.82), calls=%async_computation.4 | async-start | bytes 6291456 | tf_op jit(solution)/shard_map/all_to_all | solution.py:78
  648.7 0.9 mul.71
  649.6 0.8 reshape.96
  650.5 6.8 gather_fusion
  657.3 0.7 reshape.97
  658.0 1.4 copy.85
  659.4 29.1 %all-to-all-done.3 = bf16[32,2,24,1024]{3,2,1,0:T(8,128)(2,1)S(1)} async-done(((bf16[32,2,24,1024]{3,2,1,0:T(8,128)(2,1)}), bf16[32,2,24,1024]{3,2,1,0:T(8,128)(2,1)S(1)}, u32[]{:S(2)}, u32[]{:S(2)}) %all-to-all-start.3) | async-done | bytes 3145760 | tf_op jit(solution)/shard_map/all_to_all | solution.py:78
  688.4 1.3 convolution_convert_fusion.2
  (13 shorter events, 0.2 us)
Async XLA Ops:
  7.2 23.1 %copy-start.3 = (bf16[128,8]{0,1:T(8,128)(2,1)S(1)}, bf16[128,8]{0,1:T(8,128)(2,1)}, u32[]{:S(2)}) copy-start(bf16[128,8]{0,1:T(8,128)(2,1)} %param.9) | copy-start | bytes 6148
  7.2 24.0 %collective-permute-start = (bf16[128,1024]{1,0:T(8,128)(2,1)}, bf16[128,1024]{1,0:T(8,128)(2,1)S(1)}, u32[]{:S(2)}, u32[]{:S(2)}) collective-permute-start(bf16[128,1024]{1,0:T(8,128)(2,1)} %param.8), channel_id=1, source_target_pairs={{0,1},{1,2},{2,3},{3,0},{4,5},{5,6},{6,7},{7,4},{8,9},{9,10},{10,1... | collective-permute-start | bytes 786440 | tf_op jit(solution)/shard_map/ppermute | solution.py:13
  9.3 36.8 %collective-permute-start.2 = (bf16[128,1024]{1,0:T(8,128)(2,1)}, bf16[128,1024]{1,0:T(8,128)(2,1)S(1)}, u32[]{:S(2)}, u32[]{:S(2)}) collective-permute-start(bf16[128,1024]{1,0:T(8,128)(2,1)} %param.8), channel_id=1, source_target_pairs={{0,3},{1,0},{2,1},{3,2},{4,7},{5,4},{6,5},{7,6},{8,11},{9,8},{10,9... | collective-permute-start | bytes 786440 | tf_op jit(solution)/shard_map/ppermute | solution.py:15
  31.1 14.9 %collective-permute-start.1 = (bf16[128,1024]{1,0:T(8,128)(2,1)S(1)}, bf16[128,1024]{1,0:T(8,128)(2,1)S(1)}, u32[]{:S(2)}, u32[]{:S(2)}) collective-permute-start(bf16[128,1024]{1,0:T(8,128)(2,1)S(1)} %collective-permute-done), channel_id=1, source_target_pairs={{0,1},{1,2},{2,3},{3,0},{4,5},{5,6},{6,7},{7,4},{8,9},{9,10},{10,1... | collective-permute-start | bytes 786440 | tf_op jit(solution)/shard_map/ppermute | solution.py:13
  31.3 14.8 %copy-start.1 = (bf16[128,1024]{1,0:T(8,128)(2,1)S(1)}, bf16[128,1024]{1,0:T(8,128)(2,1)}, u32[]{:S(2)}) copy-start(bf16[128,1024]{1,0:T(8,128)(2,1)} %param.8) | copy-start | bytes 786436
  33.2 19.4 %all-to-all-start = ((bf16[32,2,24]{2,1,0:T(2,128)(2,1)}), bf16[32,2,24]{2,1,0:T(2,128)(2,1)}, u32[]{:S(2)}, u32[]{:S(2)}) async-start(bf16[32,2,24]{2,1,0:T(2,128)(2,1)} %reshape.92), calls=%async_computation | async-start | bytes 32768 | tf_op jit(solution)/shard_map/all_to_all | solution.py:55
  52.6 182.1 %all-to-all-start.1 = ((bf16[32,2,24,4096]{3,2,1,0:T(8,128)(2,1)}), bf16[32,2,24,4096]{3,2,1,0:T(8,128)(2,1)}, u32[]{:S(2)}, u32[]{:S(2)}) async-start(bf16[32,2,24,4096]{3,2,1,0:T(8,128)(2,1)} %bitcast.100), calls=%async_computation.1 | async-start | bytes 25165824 | tf_op jit(solution)/shard_map/all_to_all | solution.py:54
  60.0 26.5 %all-gather.2.cloned.1.call-start = ((), (), s32[]{:S(2)}) async-start(), calls=%async_computation.6 | async-start | bytes 1310720 | tf_op jit(solution)/shard_map/all_gather | solution.py:49
  234.7 204.3 %all-to-all-start.2 = ((bf16[32,2,24,4096]{3,2,1,0:T(8,128)(2,1)}), bf16[32,2,24,4096]{3,2,1,0:T(8,128)(2,1)}, u32[]{:S(2)}, u32[]{:S(2)}) async-start(bf16[32,2,24,4096]{3,2,1,0:T(8,128)(2,1)} %bitcast.101), calls=%async_computation.2 | async-start | bytes 25165824 | tf_op jit(solution)/shard_map/all_to_all | solution.py:53
  264.4 372.0 %reduce-scatter.2.cloned.1.call-start = ((), (), s32[]{:S(2)}) async-start(), calls=%async_computation.7 | async-start | bytes 15728640 | tf_op jit(solution)/shard_map/reduce_scatter | solution.py:74
  450.1 13.8 %copy-start = (f32[2,32,24,384]{3,2,1,0:T(8,128)}, f32[2,32,24,384]{3,2,1,0:T(8,128)S(1)}, u32[]{:S(2)}) copy-start(f32[2,32,24,384]{3,2,1,0:T(8,128)S(1)} %fusion.3) | copy-start | bytes 7077892
  512.9 127.5 %all-to-all-start.4 = ((bf16[32,2,24]{2,1,0:T(2,128)(2,1)}), bf16[32,2,24]{2,1,0:T(2,128)(2,1)S(1)}, u32[]{:S(2)}, u32[]{:S(2)}) async-start(bf16[32,2,24]{2,1,0:T(2,128)(2,1)} %copy.84), calls=%async_computation.5 | async-start | bytes 32768 | tf_op jit(solution)/shard_map/all_to_all | solution.py:79
  640.4 0.6 copy-start.2
  641.0 47.4 %all-to-all-start.3 = ((bf16[32,2,24,1024]{3,2,1,0:T(8,128)(2,1)}), bf16[32,2,24,1024]{3,2,1,0:T(8,128)(2,1)S(1)}, u32[]{:S(2)}, u32[]{:S(2)}) async-start(bf16[32,2,24,1024]{3,2,1,0:T(8,128)(2,1)} %copy.82), calls=%async_computation.4 | async-start | bytes 6291456 | tf_op jit(solution)/shard_map/all_to_all | solution.py:78
Sparse Core Ops, SparseCore 0:
  62.5 23.9 all-gather.1
  498.7 137.6 reduce-scatter.1
